TPU v7x, 32 devices: a whole 2x2x4 slice. The times are simulated.
32 devices in a mesh: groups: 2 (over y), row: 8 (over z, x), col: 2 (over core).
Axes of the slice: x: 2, y: 2, z: 4, core: 2. Of those that a mesh axis runs over, the one named last changes fastest.
Arguments:
- object_slices: float32 [4, 2, 2048, 512], P(None, None, ('groups', 'row'), 'col'), parts along dimension 2, may hold values from -4 to 4
- probe: float32 [16, 2, 128, 128], P('groups'), parts along dimension 0, may hold values from -3 to 3
- taps: float32 [2, 63], replicated, may hold values from -0.5 to 0.5
- measured: float32 [64, 128, 128], P(('groups', 'row', 'col')), parts along dimension 0, may hold values from 0.5 to 16
- positions: int32 [64, 2], P(('groups', 'row', 'col')), parts along dimension 0, may hold values from -64 to 959, as said below
Outputs:
- object_grad: float32 [4, 2, 2048, 512], P(None, None, ('groups', 'row'), 'col'), parts along dimension 2
- new_probe: float32 [16, 2, 16384], P('groups', None, ('row', 'col')), parts along dimension 0
There are 2 independent parts, one for each index of `groups`. A program takes and returns all parts, laid end to end along the dimension named above; an argument that names none is the same for every part. Nothing has to cross between parts.
Inputs may be any that keep to these rules, and one draw needn't show every extreme that they name: `positions`: record r belongs to device d = r // 2 in row-major order over the (row, col) device grid, with tile indices (i, q); its row lies in [i * 128 - 128/2, (i + 1) * 128 - 128/2) and its column in [q * 256 - 128/2, (q + 1) * 256 - 128/2).
All inputs are finite; a program needn't handle non-finite values.
Results may differ from a plain program's by a relative error of at most 0.0003.
Values sent between devices are 32-bit elements; how exact they have to be, the bound alone decides.
No kernel may reach another device: no remote copies, remote signals or barrier semaphores. Data moves between devices by JAX's collectives and lax.ppermute only.
A program may use at most 64 MiB of HBM per device.

v0:
```python
import math
import jax
import jax.numpy as jnp
from jax import lax
from jax.sharding import PartitionSpec as P

highest_mode = lax.Precision.HIGHEST


def from_behind(value, axis, steps):
    count = lax.axis_size(axis)
    first, last = (max(0, -steps), min(count, count - steps))
    return lax.ppermute(value, axis, [(source, source + steps) for source in range(first, last)])


def with_halo(array, sides, width):
    for axis, dim in sides:
        devices, length = (lax.axis_size(axis), array.shape[dim])
        up = [(i, (i + 1) % devices) for i in range(devices - 1)]
        down = [(j, i) for i, j in up]
        last = lax.slice_in_dim(array, length - width, length, axis=dim)
        first = lax.slice_in_dim(array, 0, width, axis=dim)
        before = lax.ppermute(last, axis, up)
        after = lax.ppermute(first, axis, down)
        array = jnp.concatenate([before, array, after], axis=dim)
    return array


def einsum_exact(form, first, second):
    return jnp.einsum(form, first, second, precision=highest_mode)


def make_tables(taps, width):
    reach = taps.shape[1] // 2
    pixel_idx = lax.iota(jnp.int32, width)
    offset = pixel_idx[None, :] - pixel_idx[:, None] + reach
    tap_idx = lax.iota(jnp.int32, taps.shape[1])
    one_hot = (offset[:, :, None] == tap_idx[None, None, :]).astype(jnp.float32)
    band_re = einsum_exact("abt,t->ab", one_hot, taps[0])
    band_im = einsum_exact("abt,t->ab", one_hot, taps[1])
    phase_idx = pixel_idx[:, None] * pixel_idx[None, :] % width
    angle = 2.0 * math.pi / width * phase_idx.astype(jnp.float32)
    norm_factor = 1.0 / math.sqrt(width)
    return (band_re, band_im, jnp.cos(angle) * norm_factor, -jnp.sin(angle) * norm_factor)


def both_sides(mat_re, mat_im, wave_re, wave_im):
    left_re = einsum_exact("ab,kbc->kac", mat_re, wave_re) - einsum_exact(
        "ab,kbc->kac", mat_im, wave_im
    )
    left_im = einsum_exact("ab,kbc->kac", mat_re, wave_im) + einsum_exact(
        "ab,kbc->kac", mat_im, wave_re
    )
    out_re = einsum_exact("kac,dc->kad", left_re, mat_re) - einsum_exact(
        "kac,dc->kad", left_im, mat_im
    )
    out_im = einsum_exact("kac,dc->kad", left_re, mat_im) + einsum_exact(
        "kac,dc->kad", left_im, mat_re
    )
    return (out_re, out_im)


def record_loss(probe, patch, measured_one, tables):
    band_re, band_im, dft_re, dft_im = tables
    wave_re = probe[:, 0]
    wave_im = probe[:, 1]
    layers = patch.shape[0]
    for layer_idx in range(layers):
        obj_re = patch[layer_idx, 0]
        obj_im = patch[layer_idx, 1]
        wave_re, wave_im = (
            wave_re * obj_re - wave_im * obj_im,
            wave_re * obj_im + wave_im * obj_re,
        )
        if layer_idx + 1 < layers:
            wave_re, wave_im = both_sides(band_re, band_im, wave_re, wave_im)
    far_re, far_im = both_sides(dft_re, dft_im, wave_re, wave_im)
    intensity = jnp.sum(far_re * far_re + far_im * far_im, axis=0)
    weight = 1.0 / (8.0 * probe.shape[0])
    return 0.5 * weight * jnp.sum((intensity - measured_one) ** 2)


def accumulate(grid, probe, measured, places, tables, patch_width):
    sizes = (grid.shape[0], 2, patch_width, patch_width)

    def one_record(carry, item):
        grad_grid, grad_probe = carry
        place, measured_one = item
        zero_idx = jnp.zeros((), jnp.int32)
        starts = (zero_idx, zero_idx, place[0], place[1])
        patch = lax.dynamic_slice(grid, starts, sizes)
        grad_wave, grad_patch = jax.grad(record_loss, argnums=(0, 1))(
            probe, patch, measured_one, tables
        )
        current = lax.dynamic_slice(grad_grid, starts, sizes)
        grad_grid = lax.dynamic_update_slice(grad_grid, current + grad_patch, starts)
        return ((grad_grid, grad_probe + grad_wave), None)

    init = (jnp.zeros(grid.shape, jnp.float32), jnp.zeros(probe.shape, jnp.float32))
    (grad_grid, grad_probe), unused = lax.scan(one_record, init, (places, measured))
    return (grad_grid, grad_probe)


def gram_of(first, second):
    stacked = jnp.concatenate([first, second], axis=0)
    col_re = stacked[:, 0]
    col_im = stacked[:, 1]
    gram_re = einsum_exact("ax,bx->ab", col_re, col_re) + einsum_exact("ax,bx->ab", col_im, col_im)
    gram_im = einsum_exact("ax,bx->ab", col_re, col_im) - einsum_exact("ax,bx->ab", col_im, col_re)
    return (gram_re, gram_im)


def complex_cholesky(herm_re, herm_im):
    count = herm_re.shape[0]
    order_idx = lax.iota(jnp.int32, count)
    cols_re = []
    cols_im = []
    for col_idx in range(count):
        numer_re = herm_re[:, col_idx]
        numer_im = herm_im[:, col_idx]
        for prev_idx in range(col_idx):
            vec_re = cols_re[prev_idx]
            vec_im = cols_im[prev_idx]
            pivot_re = vec_re[col_idx]
            pivot_im = vec_im[col_idx]
            numer_re = numer_re - (vec_re * pivot_re + vec_im * pivot_im)
            numer_im = numer_im - (vec_im * pivot_re - vec_re * pivot_im)
        diag_val = jnp.sqrt(numer_re[col_idx])
        below = order_idx > col_idx
        at_diag = order_idx == col_idx
        cols_re.append(
            jnp.where(below, numer_re / diag_val, 0.0) + jnp.where(at_diag, diag_val, 0.0)
        )
        cols_im.append(jnp.where(below, numer_im / diag_val, 0.0))
    return (jnp.stack(cols_re, axis=1), jnp.stack(cols_im, axis=1))


def lower_inverse(low_re, low_im):
    count = low_re.shape[0]
    unit = jnp.eye(count, dtype=low_re.dtype)
    rows_re = []
    rows_im = []
    for row_idx in range(count):
        acc_re = unit[row_idx]
        acc_im = jnp.zeros_like(unit[row_idx])
        for prev_idx in range(row_idx):
            coef_re = low_re[row_idx, prev_idx]
            coef_im = low_im[row_idx, prev_idx]
            acc_re = acc_re - (coef_re * rows_re[prev_idx] - coef_im * rows_im[prev_idx])
            acc_im = acc_im - (coef_re * rows_im[prev_idx] + coef_im * rows_re[prev_idx])
        rows_re.append(acc_re / low_re[row_idx, row_idx])
        rows_im.append(acc_im / low_re[row_idx, row_idx])
    return (jnp.stack(rows_re, axis=0), jnp.stack(rows_im, axis=0))


def orthonormalize(probe_cols, grad_cols, gram_re, gram_im, scale_out):
    modes = probe_cols.shape[0]
    trace_pp = jnp.trace(gram_re[:modes, :modes])
    trace_gg = jnp.trace(gram_re[modes:, modes:])
    factor = 0.5 * jnp.sqrt(trace_pp / (trace_gg + 1e-06))
    new_re = (
        gram_re[:modes, :modes]
        - factor * (gram_re[:modes, modes:] + gram_re[modes:, :modes])
        + factor * factor * gram_re[modes:, modes:]
    )
    new_im = (
        gram_im[:modes, :modes]
        - factor * (gram_im[:modes, modes:] + gram_im[modes:, :modes])
        + factor * factor * gram_im[modes:, modes:]
    )
    low_re, low_im = complex_cholesky(new_re, new_im)
    inv_re, inv_im = lower_inverse(low_re, low_im)
    right_re = inv_re.T
    right_im = -inv_im.T
    moved = probe_cols - factor * grad_cols
    moved_re = moved[:, 0]
    moved_im = moved[:, 1]
    out_re = einsum_exact("kx,kj->jx", moved_re, right_re) - einsum_exact(
        "kx,kj->jx", moved_im, right_im
    )
    out_im = einsum_exact("kx,kj->jx", moved_re, right_im) + einsum_exact(
        "kx,kj->jx", moved_im, right_re
    )
    return jnp.stack([out_re, out_im], axis=1) * scale_out


def fold_axis(grad, dim, half):
    full = grad.shape[dim]
    inner = full - 2 * half
    core = lax.slice_in_dim(grad, half, half + inner, axis=dim)
    for step_by in (1, -1):
        if step_by == 1:
            sent = lax.slice_in_dim(grad, half + inner, full, axis=dim)
        else:
            sent = lax.slice_in_dim(grad, 0, half, axis=dim)
        if dim == 2:
            arrived = from_behind(sent, "row", step_by)
        else:
            arrived = from_behind(sent, "col", step_by)
        widths = [(0, 0)] * grad.ndim
        if step_by == 1:
            widths[dim] = (0, inner - half)
        else:
            widths[dim] = (inner - half, 0)
        core = core + jnp.pad(arrived, widths)
    return core


def per_device(object_slices, probe, taps, measured, positions):
    width = probe.shape[-1]
    half = width // 2
    tile_rows = object_slices.shape[2]
    tile_cols = object_slices.shape[3]
    tables = make_tables(taps, width)
    extended = with_halo(object_slices, (("row", 2), ("col", 3)), half)
    anchor = jnp.stack(
        [lax.axis_index("row") * tile_rows - half, lax.axis_index("col") * tile_cols - half]
    )
    places = positions - anchor[None, :]
    grad_ext, grad_probe = accumulate(extended, probe, measured, places, tables, width)
    folded = fold_axis(fold_axis(grad_ext, 2, half), 3, half)
    modes = probe.shape[0]
    pixels = width * width
    probe_cols = probe.reshape(modes, 2, pixels)
    grad_cols = grad_probe.reshape(modes, 2, pixels)
    share = pixels // (lax.axis_size("row") * lax.axis_size("col"))
    start = lax.axis_index(("row", "col")) * share
    own_probe = lax.dynamic_slice_in_dim(probe_cols, start, share, 2)
    total_grad = lax.psum(grad_cols, ("row", "col"))
    gram_re, gram_im = gram_of(probe_cols, total_grad)
    own_grad = lax.dynamic_slice_in_dim(total_grad, start, share, 2)
    new_probe = orthonormalize(own_probe, own_grad, gram_re, gram_im, float(width))
    return (folded, new_probe)


def solution(mesh):
    placed = (
        P(None, None, ("groups", "row"), "col"),
        P("groups", None, None, None),
        P(),
        P(("groups", "row", "col"), None, None),
        P(("groups", "row", "col"), None),
    )
    return jax.shard_map(
        per_device,
        mesh=mesh,
        in_specs=placed,
        out_specs=(P(None, None, ("groups", "row"), "col"), P("groups", None, ("row", "col"))),
        check_vma=False,
    )
```

profile of v0, /device:TPU:0, one launch (start us, length us, event | category | flops | bytes accessed | tf_op | source)
XLA Modules:
  0.0 651.3 jit_solution(16764180511014686650)
XLA Ops:
  8.5 4.9 collective-permute-start
  18.0 17.8 %collective-permute-done = f32[4,2,64,256]{3,2,1,0:T(8,128)S(1)} collective-permute-done((f32[4,2,64,256]{3,2,1,0:T(8,128)S(1)}, f32[4,2,64,256]{3,2,1,0:T(8,128)S(1)}, u32[]{:S(2)}, u32[]{:S(2)}) %collective-permute-start) | collective-permute-done | bytes 524320 | tf_op jit(solution)/shard_map/ppermute | solution.py:23
  44.0 3.3 fusion.235
  47.3 3.2 fusion.233
  50.5 3.8 pad_maximum_fusion
  56.2 173.7 %while.16 = (s32[]{:T(128)}, f32[4,2,256,384]{3,2,1,0:T(8,128)}, f32[8,2,128,128]{2,3,0,1:T(8,128)}, s32[2,2]{1,0:T(2,128)S(1)}, f32[8,2,128,128]{2,3,0,1:T(8,12...) while((s32[]{:T(128)}, f32[4,2,256,384]{3,2,1,0:T(8,128)}, ...), condition=%wide.region_18.19_spmd.clone.clone, body=%wide.region_0.18_spmd.clone.clone.sunk | while | flops 12914802688 | bytes 137233312 | solution.py:100
  131.2 7.7 %dynamic_update_slice.9 = f32[4,2,256,384]{3,2,1,0:T(8,128)} dynamic-update-slice(f32[4,2,256,384]{3,2,1,0:T(8,128)} %get-tuple-element.615, f32[4,2,128,128]{3,2,1,0:T(8,128)S(1)} %add_add_fusion.2, s32[]{:T(128)} %constant.94.clone.1..sunk, s32[]{:T(128)} %constant.94.clone.1..sunk, s32[]{:T(128)S(6)} %select_n.471, s32[]{:T(128)S(6)} %select_n.472) | dynamic-update-slice | bytes 1048580 | tf_op jit(solution)/shard_map/while/body/eval_jaxpr/dynamic_update_slice | solution.py:96
  210.7 2.4 select_add_fusion.2
  215.2 7.2 %dynamic_update_slice.9 = f32[4,2,256,384]{3,2,1,0:T(8,128)} dynamic-update-slice(f32[4,2,256,384]{3,2,1,0:T(8,128)} %get-tuple-element.615, f32[4,2,128,128]{3,2,1,0:T(8,128)S(1)} %add_add_fusion.2, s32[]{:T(128)} %constant.94.clone.1..sunk, s32[]{:T(128)} %constant.94.clone.1..sunk, s32[]{:T(128)S(6)} %select_n.471, s32[]{:T(128)S(6)} %select_n.472) | dynamic-update-slice | bytes 1048580 | tf_op jit(solution)/shard_map/while/body/eval_jaxpr/dynamic_update_slice | solution.py:96
  233.4 2.7 fusion.298
  236.1 5.0 collective-permute-start.4
  242.4 91.3 %all-reduce.16.cloned.1.call-done = f32[8,2,16384]{2,0,1:T(8,128)} async-done(((f32[8,2,16384]{2,0,1:T(8,128)}), f32[8,2,16384]{2,0,1:T(8,128)}) %all-reduce.16.cloned.1.call-update) | async-done | bytes 1048592 | tf_op jit(solution)/shard_map/psum | solution.py:229
  333.7 2.7 fusion.295
  336.4 2.7 convolution_add_fusion.25
  363.4 3.8 fusion.286
  368.6 3.8 compare_select_fusion.15
  375.1 5.0 fusion.282
  381.5 5.1 compare_select_fusion.13
  389.2 6.2 add_subtract_fusion.2
  396.6 6.2 compare_select_fusion.11
  405.3 7.6 %add_subtract_fusion.1 = f32[8]{0:T(128)S(1)} fusion(f32[8]{0:T(128)S(1)} %compare_select_fusion.11, f32[8]{0:T(128)S(1)} %compare_select_fusion.13, f32[8]{0:T(128)S(1)} %compare_select_fusion.15, f32[8]{0:T(128)S(1)} %compare_select_fusion.17, f32[8]{0:T(128)S(1)} %compare_select_fusion.19, f32[8]{0:T(128)S(1)} %get-tuple-element.459, ...), kind=kLoop, calls=%fused_computation.455 | loop fusion | flops 432 | bytes 516 | tf_op jit(solution)/shard_map/sub | solution.py:126
  414.2 7.6 %compare_select_fusion.9 = f32[8]{0:T(128)S(1)} fusion(f32[8]{0:T(128)S(1)} %compare_select_fusion.11, f32[8]{0:T(128)S(1)} %compare_select_fusion.13, f32[8]{0:T(128)S(1)} %compare_select_fusion.15, f32[8]{0:T(128)S(1)} %compare_select_fusion.17, f32[8]{0:T(128)S(1)} %compare_select_fusion.19, f32[8]{0:T(128)S(1)} %get-tuple-element.460, ...), kind=kLoop, calls=%fused_computation.391 | loop fusion | flops 456 | bytes 520 | tf_op jit(solution)/shard_map/jit(_where)/select_n | solution.py:134
  423.6 8.8 %add_subtract_fusion = f32[8]{0:T(128)S(1)} fusion(f32[8]{0:T(128)S(1)} %compare_select_fusion.9, f32[8]{0:T(128)S(1)} %compare_select_fusion.11, f32[8]{0:T(128)S(1)} %compare_select_fusion.13, f32[8]{0:T(128)S(1)} %compare_select_fusion.15, f32[8]{0:T(128)S(1)} %compare_select_fusion.17, f32[8]{0:T(128)S(1)} %compare_select_fusion.19, ...), kind=kLoop, calls=%fused_computation.454 | loop fusion | flops 512 | bytes 592 | tf_op jit(solution)/shard_map/sub | solution.py:126
  434.1 39.2 %subtract_divide_fusion.1 = (f32[1,8]{0,1:T(8,128)S(1)}, f32[1,8]{0,1:T(8,128)S(1)}, f32[1,8]{0,1:T(8,128)S(1)}, f32[1,8]{0,1:T(8,128)S(1)}, f32[1,8]{0,1:T(8,128)S(1)}) fusion(f32[8,8]{0,1:T(8,128)S(1)} %fusion.251, f32[]{:T(128)} %bitcast.99, f32[]{:T(128)} %bitcast.67, f32[]{:T(128)S(6)} %mul.2504, f32[]{:T(128)} %bitcast.96, f32[]{:T(128)} %bitcast.94, ...), kind=kLoop, calls=%fused_computation.360 | loop fusion | flops 1576 | bytes 720 | tf_op jit(solution)/shard_map/div | solution.py:151
  473.4 27.4 %subtract_divide_fusion.3 = f32[1,8]{0,1:T(8,128)S(1)} fusion(f32[]{:T(128)} %bitcast.81, f32[1,8]{0,1:T(8,128)S(1)} %get-tuple-element.353, f32[1,8]{0,1:T(8,128)S(1)} %get-tuple-element.354, f32[1,8]{0,1:T(8,128)S(1)} %get-tuple-element.355, f32[1,8]{0,1:T(8,128)S(1)} %get-tuple-element.356, f32[]{:T(128)} %bitcast.53, f32[8,8]{0,1:T(8,128)S(1)} %fusion.251, ...), kind=kLoop, calls=%fused_computation.362 | loop fusion | flops 960 | bytes 464 | tf_op jit(solution)/shard_map/div | solution.py:151
  500.8 19.0 %subtract_divide_fusion.5 = f32[1,8]{0,1:T(8,128)S(1)} fusion(f32[1,8]{0,1:T(8,128)S(1)} %get-tuple-element.354, f32[1,8]{0,1:T(8,128)S(1)} %get-tuple-element.355, f32[1,8]{0,1:T(8,128)S(1)} %get-tuple-element.356, f32[1,8]{0,1:T(8,128)S(1)} %get-tuple-element.353, f32[8,8]{0,1:T(8,128)S(1)} %fusion.251, f32[]{:T(128)} %bitcast.65, f32[]{:T(128)} %bitcast.41, ...), kind=kLoop, calls=%fused_computation.365 | loop fusion | flops 608 | bytes 372 | tf_op jit(solution)/shard_map/div | solution.py:151
  519.8 12.3 %subtract_divide_fusion.7 = f32[1,8]{0,1:T(8,128)S(1)} fusion(f32[1,8]{0,1:T(8,128)S(1)} %get-tuple-element.353, f32[1,8]{0,1:T(8,128)S(1)} %get-tuple-element.354, f32[1,8]{0,1:T(8,128)S(1)} %get-tuple-element.355, f32[1,8]{0,1:T(8,128)S(1)} %get-tuple-element.356, f32[8,8]{0,1:T(8,128)S(1)} %fusion.251, f32[]{:T(128)} %bitcast.51, f32[]{:T(128)} %bitcast.31, ...), kind=kLoop, calls=%fused_computation.368 | loop fusion | flops 320 | bytes 288 | tf_op jit(solution)/shard_map/div | solution.py:151
  532.7 27.3 %subtract_divide_fusion.2 = f32[1,8]{0,1:T(8,128)S(1)} fusion(f32[1,8]{0,1:T(8,128)S(1)} %get-tuple-element.353, f32[1,8]{0,1:T(8,128)S(1)} %get-tuple-element.354, f32[1,8]{0,1:T(8,128)S(1)} %get-tuple-element.355, f32[1,8]{0,1:T(8,128)S(1)} %get-tuple-element.356, f32[]{:T(128)} %bitcast.67, f32[]{:T(128)S(6)} %mul.2504, f32[]{:T(128)} %bitcast.81, ...), kind=kLoop, calls=%fused_computation.361 | loop fusion | flops 960 | bytes 432 | tf_op jit(solution)/shard_map/div | solution.py:152
  559.9 19.0 %subtract_divide_fusion.4 = f32[1,8]{0,1:T(8,128)S(1)} fusion(f32[1,8]{0,1:T(8,128)S(1)} %get-tuple-element.353, f32[1,8]{0,1:T(8,128)S(1)} %get-tuple-element.354, f32[1,8]{0,1:T(8,128)S(1)} %get-tuple-element.355, f32[1,8]{0,1:T(8,128)S(1)} %get-tuple-element.356, f32[]{:T(128)} %bitcast.53, f32[]{:T(128)S(6)} %mul.2430, f32[]{:T(128)} %bitcast.65, ...), kind=kLoop, calls=%fused_computation.363 | loop fusion | flops 608 | bytes 340 | tf_op jit(solution)/shard_map/div | solution.py:152
  578.9 7.2 %subtract_divide_fusion.8 = (f32[1,8]{0,1:T(8,128)S(1)}, f32[1,8]{0,1:T(8,128)S(1)}, f32[1,8]{0,1:T(8,128)S(1)}) fusion(f32[1,8]{0,1:T(8,128)S(1)} %get-tuple-element.354, f32[1,8]{0,1:T(8,128)S(1)} %get-tuple-element.355, f32[1,8]{0,1:T(8,128)S(1)} %get-tuple-element.356, f32[]{:T(128)} %bitcast.31, f32[]{:T(128)S(6)} %mul.2318, f32[]{:T(128)} %bitcast.39, ...), kind=kLoop, calls=%fused_computation.369 | loop fusion | flops 192 | bytes 252 | tf_op jit(solution)/shard_map/div | solution.py:152
  586.1 36.6 %subtract_divide_fusion = f32[1,8]{0,1:T(8,128)S(1)} fusion(f32[1,8]{0,1:T(8,128)S(1)} %get-tuple-element.353, f32[1,8]{0,1:T(8,128)S(1)} %get-tuple-element.354, f32[1,8]{0,1:T(8,128)S(1)} %get-tuple-element.355, f32[1,8]{0,1:T(8,128)S(1)} %get-tuple-element.356, f32[]{:T(128)} %bitcast.83, f32[]{:T(128)S(6)} %mul.2550, f32[]{:T(128)} %bitcast.99, ...), kind=kLoop, calls=%fused_computation.359 | loop fusion | flops 1376 | bytes 532 | tf_op jit(solution)/shard_map/div | solution.py:152
  622.8 12.2 %subtract_divide_fusion.6 = f32[1,8]{0,1:T(8,128)S(1)} fusion(f32[1,8]{0,1:T(8,128)S(1)} %get-tuple-element.353, f32[1,8]{0,1:T(8,128)S(1)} %get-tuple-element.354, f32[1,8]{0,1:T(8,128)S(1)} %get-tuple-element.355, f32[1,8]{0,1:T(8,128)S(1)} %get-tuple-element.356, f32[]{:T(128)} %bitcast.41, f32[]{:T(128)S(6)} %mul.2368, f32[]{:T(128)} %bitcast.51, ...), kind=kLoop, calls=%fused_computation.366 | loop fusion | flops 320 | bytes 256 | tf_op jit(solution)/shard_map/div | solution.py:152
  (339 shorter events, 193.8 us)
Async XLA Ops:
  7.2 326.5 %all-reduce.16.cloned.1.call-start = ((), (), s32[]{:S(2)}) async-start(), calls=%async_computation | async-start | bytes 2097152 | tf_op jit(solution)/shard_map/psum | solution.py:229
  8.5 27.2 %collective-permute-start = (f32[4,2,64,256]{3,2,1,0:T(8,128)S(1)}, f32[4,2,64,256]{3,2,1,0:T(8,128)S(1)}, u32[]{:S(2)}, u32[]{:S(2)}) collective-permute-start(f32[4,2,64,256]{3,2,1,0:T(8,128)S(1)} %get-tuple-element.392), channel_id=1, source_target_pairs={{0,2},{2,4},{4,6},{6,8},{8,10},{10,12},{12,14},{1,3},{3,5},{5,7},{... | collective-permute-start | bytes 1572872 | tf_op jit(solution)/shard_map/ppermute | solution.py:23
  13.4 22.7 %collective-permute-start.1 = (f32[4,2,64,256]{3,2,1,0:T(8,128)S(1)}, f32[4,2,64,256]{3,2,1,0:T(8,128)}, u32[]{:S(2)}, u32[]{:S(2)}) collective-permute-start(f32[4,2,64,256]{3,2,1,0:T(8,128)S(1)} %get-tuple-element.393), channel_id=1, source_target_pairs={{2,0},{4,2},{6,4},{8,6},{10,8},{12,10},{14,12},{3,1},{5,3},{7,5},{... | collective-permute-start | bytes 1572872 | tf_op jit(solution)/shard_map/ppermute | solution.py:24
  36.1 6.2 copy-start.23
  37.5 4.9 copy-start.9
  37.5 6.4 copy-start.24
  39.0 11.5 %collective-permute-start.2 = (f32[4,2,256,64]{2,3,1,0:T(8,128)}, f32[4,2,256,64]{2,3,1,0:T(8,128)}, u32[]{:S(2)}, u32[]{:S(2)}) collective-permute-start(f32[4,2,256,64]{2,3,1,0:T(8,128)} %get-tuple-element.388), channel_id=1, source_target_pairs={{0,1},{2,3},{4,5},{6,7},{8,9},{10,11},{12,13},{14,15},{16,17},{18,... | collective-permute-start | bytes 1572872 | tf_op jit(solution)/shard_map/ppermute | solution.py:23
  41.1 9.5 %collective-permute-start.3 = (f32[4,2,256,64]{2,3,1,0:T(8,128)}, f32[4,2,256,64]{2,3,1,0:T(8,128)}, u32[]{:S(2)}, u32[]{:S(2)}) collective-permute-start(f32[4,2,256,64]{2,3,1,0:T(8,128)} %get-tuple-element.389), channel_id=1, source_target_pairs={{1,0},{3,2},{5,4},{7,6},{9,8},{11,10},{13,12},{15,14},{17,16},{19,... | collective-permute-start | bytes 1572872 | tf_op jit(solution)/shard_map/ppermute | solution.py:24
  44.0 6.6 %copy-start.10 = (f32[4,2,64,256]{2,3,1,0:T(8,128)S(1)}, f32[4,2,64,256]{2,3,1,0:T(8,128)}, u32[]{:S(2)}) copy-start(f32[4,2,64,256]{2,3,1,0:T(8,128)} %copy-done.9) | copy-start | bytes 1572868
  56.7 9.2 %copy-start = (f32[8,2,128,128]{2,3,0,1:T(8,128)}, f32[8,2,128,128]{2,3,0,1:T(8,128)S(1)}, u32[]{:S(2)}) copy-start(f32[8,2,128,128]{2,3,0,1:T(8,128)S(1)} %get-tuple-element.634) | copy-start | bytes 3145732 | tf_op jit(solution)/shard_map/while
  63.6 3.4 copy-start.6
  90.6 4.4 copy-start.2
  90.6 4.4 copy-start.3
  97.4 4.5 copy-start.22
  123.2 3.6 copy-start.5
  123.2 3.6 copy-start.7
  139.2 9.2 %copy-start = (f32[8,2,128,128]{2,3,0,1:T(8,128)}, f32[8,2,128,128]{2,3,0,1:T(8,128)S(1)}, u32[]{:S(2)}) copy-start(f32[8,2,128,128]{2,3,0,1:T(8,128)S(1)} %get-tuple-element.634) | copy-start | bytes 3145732 | tf_op jit(solution)/shard_map/while
  146.0 3.4 copy-start.6
  173.3 4.4 copy-start.2
  173.3 4.4 copy-start.3
  180.0 4.5 copy-start.22
  205.9 3.6 copy-start.5
  205.9 3.6 copy-start.7
  209.5 3.7 copy-start.11
  209.5 3.7 copy-start.12
  209.6 3.7 copy-start.13
  209.6 3.7 copy-start.14
  236.1 399.5 %collective-permute-start.4 = (f32[4,2,64,384]{3,2,1,0:T(8,128)}, f32[4,2,64,384]{3,2,1,0:T(8,128)S(1)}, u32[]{:S(2)}, u32[]{:S(2)}) collective-permute-start(f32[4,2,64,384]{3,2,1,0:T(8,128)} %get-tuple-element.386), channel_id=1, source_target_pairs={{0,2},{2,4},{4,6},{6,8},{8,10},{10,12},{12,14},{1,3},{3,5},{5,7},{... | collective-permute-start | bytes 2359304 | tf_op jit(solution)/shard_map/ppermute | solution.py:13
  241.1 394.5 %collective-permute-start.5 = (f32[4,2,64,384]{3,2,1,0:T(8,128)}, f32[4,2,64,384]{3,2,1,0:T(8,128)}, u32[]{:S(2)}, u32[]{:S(2)}) collective-permute-start(f32[4,2,64,384]{3,2,1,0:T(8,128)} %get-tuple-element.387), channel_id=1, source_target_pairs={{2,0},{4,2},{6,4},{8,6},{10,8},{12,10},{14,12},{3,1},{5,3},{7,5},{... | collective-permute-start | bytes 2359304 | tf_op jit(solution)/shard_map/ppermute | solution.py:13
  333.7 8.8 %copy-start.8 = (f32[8,2,16384]{2,0,1:T(8,128)S(1)}, f32[8,2,16384]{2,0,1:T(8,128)}, u32[]{:S(2)}) copy-start(f32[8,2,16384]{2,0,1:T(8,128)} %all-reduce.16.cloned.1.call-done) | copy-start | bytes 3145732
  637.7 3.8 collective-permute-start.6
  639.0 3.8 collective-permute-start.7
  (21 other events, 47.2 us)
Sparse Core Ops, SparseCore 0:
  232.9 100.7 all-reduce.15
where the time goes:
time: 663 us; the launch traced here: 651 us
  other arithmetic  279 us (42%)
  matrix products  135 us (20%)
  waiting for transfers between devices  110 us (17%)
  local copies, waits for them, and re-layouts  59.8 us (9%)
  between operations  30.9 us (5%)
  starting transfers between devices  18.4 us (3%)
  loops' own time  17.8 us (3%)
    dot_general x138, matrix products, einsum_exact(): return jnp.einsum(form, first, second, precision=highest_mode)  135 us
    div x5, other arithmetic, lower_inverse(): rows_im.append(acc_im / low_re[row_idx, row_idx])  102 us
    div x4, other arithmetic, lower_inverse(): rows_re.append(acc_re / low_re[row_idx, row_idx])  97.9 us
    psum x1, waiting for transfers between devices, per_device(): total_grad = lax.psum(grad_cols, ('row', 'col'))  91.3 us
    sub x7, other arithmetic, complex_cholesky(): numer_re = numer_re - (vec_re * pivot_re + vec_im * pivot_im)  34.9 us
    select_n x7, other arithmetic, complex_cholesky(): cols_im.append(jnp.where(below, numer_im / diag_val, 0.0))  26.1 us
    another operation x1, loops' own time, accumulate(): lax.scan(one_record, init, (places, measured))  17.8 us
    ppermute x2, waiting for transfers between devices, with_halo(): before = lax.ppermute(last, axis, up)  17.8 us
  transfers between devices with their start and end apart: 9, of which 3 were waited for; matrix products, arithmetic and copies ran while one was open for 46% of the time, Pallas kernels for 0%

commit v1 on v0

--- a/solution.py
+++ b/solution.py
@@ -226,7 +226,7 @@
     share = pixels // (lax.axis_size("row") * lax.axis_size("col"))
     start = lax.axis_index(("row", "col")) * share
     own_probe = lax.dynamic_slice_in_dim(probe_cols, start, share, 2)
-    total_grad = lax.psum(grad_cols, ("row", "col"))
+    total_grad = jnp.sum(lax.all_gather(grad_cols, ("row", "col")), axis=0)
     gram_re, gram_im = gram_of(probe_cols, total_grad)
     own_grad = lax.dynamic_slice_in_dim(total_grad, start, share, 2)
     new_probe = orthonormalize(own_probe, own_grad, gram_re, gram_im, float(width))

time: 663 us -> 706 us (1.065)
  waiting for transfers between devices: 110 us -> 146 us
  other arithmetic: 279 us -> 287 us
    psum x1 -> x0, waiting for transfers between devices: 91.3 us -> none  [per_device(): total_grad = lax.psum(grad_cols, ('row', 'col'))]
    all_gather x0 -> x1, waiting for transfers between devices: none -> 86.4 us  [per_device(): total_grad = jnp.sum(lax.all_gather(grad_cols, ('row', 'col')), axis=0)]
    ppermute x4, waiting for transfers between devices: 1.35 us -> 43.1 us  [from_behind(): lax.ppermute(value, axis, [(source, source + steps) for source in range(f...]
  transfers between devices with their start and end apart: 9 -> 9, of which waited for: 3 -> 6; matrix products, arithmetic and copies ran while one was open for 46% -> 2% of each run, Pallas kernels for 0% -> 0%
where the time goes in v1:
time: 706 us; the launch traced here: 695 us
  other arithmetic  287 us (41%)
  waiting for transfers between devices  146 us (21%)
  matrix products  130 us (18%)
  local copies, waits for them, and re-layouts  58.2 us (8%)
  between operations  30.8 us (4%)
  starting transfers between devices  25 us (4%)
  loops' own time  18.3 us (3%)
    dot_general x138, matrix products, einsum_exact(): return jnp.einsum(form, first, second, precision=highest_mode)  130 us
    div x5, other arithmetic, lower_inverse(): rows_im.append(acc_im / low_re[row_idx, row_idx])  103 us
    div x4, other arithmetic, lower_inverse(): rows_re.append(acc_re / low_re[row_idx, row_idx])  98.3 us
    all_gather x1, waiting for transfers between devices, per_device(): total_grad = jnp.sum(lax.all_gather(grad_cols, ('row', 'col')), axis=0)  86.4 us
    ppermute x4, waiting for transfers between devices, from_behind(): lax.ppermute(value, axis, [(source, source + steps) for source in range(f...  43.1 us
    sub x7, other arithmetic, complex_cholesky(): numer_re = numer_re - (vec_re * pivot_re + vec_im * pivot_im)  35.1 us
    select_n x7, other arithmetic, complex_cholesky(): cols_im.append(jnp.where(below, numer_im / diag_val, 0.0))  26.1 us
    another operation x1, loops' own time, accumulate(): lax.scan(one_record, init, (places, measured))  18.3 us
  transfers between devices with their start and end apart: 9, of which 6 were waited for; matrix products, arithmetic and copies ran while one was open for 2% of the time, Pallas kernels for 0%

profile of v1, /device:TPU:0, one launch (start us, length us, event | category | flops | bytes accessed | tf_op | source)
XLA Modules:
  0.0 695.2 jit_solution(5207896359924296557)
XLA Ops:
  9.8 6.3 collective-permute-start
  19.4 5.9 collective-permute-done.1
  25.6 11.0 %collective-permute-done = f32[4,2,64,256]{3,2,1,0:T(8,128)} collective-permute-done((f32[4,2,64,256]{3,2,1,0:T(8,128)S(1)}, f32[4,2,64,256]{3,2,1,0:T(8,128)}, u32[]{:S(2)}, u32[]{:S(2)}) %collective-permute-start) | collective-permute-done | bytes 524320 | tf_op jit(solution)/shard_map/ppermute | solution.py:23
  40.8 4.6 collective-permute-start.2
  47.0 3.3 fusion.235
  53.6 3.8 pad_maximum_fusion
  59.2 169.8 %while.16 = (s32[]{:T(128)}, f32[4,2,256,384]{3,2,1,0:T(8,128)}, f32[8,2,128,128]{2,3,0,1:T(8,128)}, s32[2,2]{1,0:T(2,128)S(1)}, f32[8,2,128,128]{2,3,0,1:T(8,12...) while((s32[]{:T(128)}, f32[4,2,256,384]{3,2,1,0:T(8,128)}, ...), condition=%wide.region_18.19_spmd.clone.clone, body=%wide.region_0.18_spmd.clone.clone.sunk | while | flops 12914802688 | bytes 135660272 | solution.py:100
  130.9 7.8 %dynamic_update_slice.9 = f32[4,2,256,384]{3,2,1,0:T(8,128)} dynamic-update-slice(f32[4,2,256,384]{3,2,1,0:T(8,128)} %get-tuple-element.615, f32[4,2,128,128]{3,2,1,0:T(8,128)S(1)} %add_add_fusion.2, s32[]{:T(128)} %constant.94.clone.1..sunk, s32[]{:T(128)} %constant.94.clone.1..sunk, s32[]{:T(128)S(6)} %select_n.471, s32[]{:T(128)S(6)} %select_n.472) | dynamic-update-slice | bytes 1048580 | tf_op jit(solution)/shard_map/while/body/eval_jaxpr/dynamic_update_slice | solution.py:96
  211.4 7.2 %dynamic_update_slice.9 = f32[4,2,256,384]{3,2,1,0:T(8,128)} dynamic-update-slice(f32[4,2,256,384]{3,2,1,0:T(8,128)} %get-tuple-element.615, f32[4,2,128,128]{3,2,1,0:T(8,128)S(1)} %add_add_fusion.2, s32[]{:T(128)} %constant.94.clone.1..sunk, s32[]{:T(128)} %constant.94.clone.1..sunk, s32[]{:T(128)S(6)} %select_n.471, s32[]{:T(128)S(6)} %select_n.472) | dynamic-update-slice | bytes 1048580 | tf_op jit(solution)/shard_map/while/body/eval_jaxpr/dynamic_update_slice | solution.py:96
  235.6 5.8 collective-permute-start.4
  241.4 24.5 %collective-permute-done.5 = f32[4,2,64,384]{3,2,1,0:T(8,128)S(1)} collective-permute-done((f32[4,2,64,384]{3,2,1,0:T(8,128)S(1)}, f32[4,2,64,384]{3,2,1,0:T(8,128)S(1)}, u32[]{:S(2)}, u32[]{:S(2)}) %collective-permute-start.5) | collective-permute-done | bytes 786464 | tf_op jit(solution)/shard_map/ppermute | solution.py:13
  265.9 17.7 %collective-permute-done.4 = f32[4,2,64,384]{3,2,1,0:T(8,128)S(1)} collective-permute-done((f32[4,2,64,384]{3,2,1,0:T(8,128)S(1)}, f32[4,2,64,384]{3,2,1,0:T(8,128)S(1)}, u32[]{:S(2)}, u32[]{:S(2)}) %collective-permute-start.4) | collective-permute-done | bytes 786464 | tf_op jit(solution)/shard_map/ppermute | solution.py:13
  292.9 86.4 %all-gather.2.cloned.1.call-done = f32[16,8,2,16384]{3,1,2,0:T(8,128)} async-done(((f32[1,8,2,16384]{3,1,2,0:T(8,128)}), f32[16,8,2,16384]{3,1,2,0:T(8,128)}) %all-gather.2.cloned.1.call-update) | async-done | bytes 16777232 | tf_op jit(solution)/shard_map/all_gather | solution.py:229
  379.3 6.6 reduce_sum.293
  409.3 3.6 fusion.286
  414.3 3.6 compare_select_fusion.15
  419.3 5.2 fusion.282
  425.8 5.2 compare_select_fusion.13
  432.3 6.0 add_subtract_fusion.2
  439.6 6.0 compare_select_fusion.11
  447.0 7.5 %add_subtract_fusion.1 = f32[8]{0:T(128)S(1)} fusion(f32[8]{0:T(128)S(1)} %compare_select_fusion.11, f32[8]{0:T(128)S(1)} %compare_select_fusion.13, f32[8]{0:T(128)S(1)} %compare_select_fusion.15, f32[8]{0:T(128)S(1)} %compare_select_fusion.17, f32[8]{0:T(128)S(1)} %compare_select_fusion.19, f32[8]{0:T(128)S(1)} %get-tuple-element.459, ...), kind=kLoop, calls=%fused_computation.455 | loop fusion | flops 432 | bytes 516 | tf_op jit(solution)/shard_map/sub | solution.py:126
  455.8 7.5 %compare_select_fusion.9 = f32[8]{0:T(128)S(1)} fusion(f32[8]{0:T(128)S(1)} %compare_select_fusion.11, f32[8]{0:T(128)S(1)} %compare_select_fusion.13, f32[8]{0:T(128)S(1)} %compare_select_fusion.15, f32[8]{0:T(128)S(1)} %compare_select_fusion.17, f32[8]{0:T(128)S(1)} %compare_select_fusion.19, f32[8]{0:T(128)S(1)} %get-tuple-element.460, ...), kind=kLoop, calls=%fused_computation.391 | loop fusion | flops 456 | bytes 520 | tf_op jit(solution)/shard_map/jit(_where)/select_n | solution.py:134
  473.2 9.0 %add_subtract_fusion = f32[8]{0:T(128)S(1)} fusion(f32[8]{0:T(128)S(1)} %compare_select_fusion.9, f32[8]{0:T(128)S(1)} %compare_select_fusion.11, f32[8]{0:T(128)S(1)} %compare_select_fusion.13, f32[8]{0:T(128)S(1)} %compare_select_fusion.15, f32[8]{0:T(128)S(1)} %compare_select_fusion.17, f32[8]{0:T(128)S(1)} %compare_select_fusion.19, ...), kind=kLoop, calls=%fused_computation.454 | loop fusion | flops 512 | bytes 592 | tf_op jit(solution)/shard_map/sub | solution.py:126
  484.2 39.3 %subtract_divide_fusion.1 = (f32[1,8]{0,1:T(8,128)S(1)}, f32[1,8]{0,1:T(8,128)S(1)}, f32[1,8]{0,1:T(8,128)S(1)}, f32[1,8]{0,1:T(8,128)S(1)}, f32[1,8]{0,1:T(8,128)S(1)}) fusion(f32[8,8]{0,1:T(8,128)S(1)} %fusion.251, f32[]{:T(128)} %bitcast.99, f32[]{:T(128)} %bitcast.67, f32[]{:T(128)S(6)} %mul.2504, f32[]{:T(128)} %bitcast.96, f32[]{:T(128)} %bitcast.94, ...), kind=kLoop, calls=%fused_computation.360 | loop fusion | flops 1576 | bytes 720 | tf_op jit(solution)/shard_map/div | solution.py:151
  523.6 7.3 %subtract_divide_fusion.8 = (f32[1,8]{0,1:T(8,128)S(1)}, f32[1,8]{0,1:T(8,128)S(1)}, f32[1,8]{0,1:T(8,128)S(1)}) fusion(f32[1,8]{0,1:T(8,128)S(1)} %get-tuple-element.354, f32[1,8]{0,1:T(8,128)S(1)} %get-tuple-element.355, f32[1,8]{0,1:T(8,128)S(1)} %get-tuple-element.356, f32[]{:T(128)} %bitcast.31, f32[]{:T(128)S(6)} %mul.2318, f32[]{:T(128)} %bitcast.39, ...), kind=kLoop, calls=%fused_computation.369 | loop fusion | flops 192 | bytes 252 | tf_op jit(solution)/shard_map/div | solution.py:152
  530.9 12.5 %subtract_divide_fusion.6 = f32[1,8]{0,1:T(8,128)S(1)} fusion(f32[1,8]{0,1:T(8,128)S(1)} %get-tuple-element.353, f32[1,8]{0,1:T(8,128)S(1)} %get-tuple-element.354, f32[1,8]{0,1:T(8,128)S(1)} %get-tuple-element.355, f32[1,8]{0,1:T(8,128)S(1)} %get-tuple-element.356, f32[]{:T(128)} %bitcast.41, f32[]{:T(128)S(6)} %mul.2368, f32[]{:T(128)} %bitcast.51, ...), kind=kLoop, calls=%fused_computation.366 | loop fusion | flops 320 | bytes 256 | tf_op jit(solution)/shard_map/div | solution.py:152
  543.4 19.2 %subtract_divide_fusion.4 = f32[1,8]{0,1:T(8,128)S(1)} fusion(f32[1,8]{0,1:T(8,128)S(1)} %get-tuple-element.353, f32[1,8]{0,1:T(8,128)S(1)} %get-tuple-element.354, f32[1,8]{0,1:T(8,128)S(1)} %get-tuple-element.355, f32[1,8]{0,1:T(8,128)S(1)} %get-tuple-element.356, f32[]{:T(128)} %bitcast.53, f32[]{:T(128)S(6)} %mul.2430, f32[]{:T(128)} %bitcast.65, ...), kind=kLoop, calls=%fused_computation.363 | loop fusion | flops 608 | bytes 340 | tf_op jit(solution)/shard_map/div | solution.py:152
  562.6 27.2 %subtract_divide_fusion.2 = f32[1,8]{0,1:T(8,128)S(1)} fusion(f32[1,8]{0,1:T(8,128)S(1)} %get-tuple-element.353, f32[1,8]{0,1:T(8,128)S(1)} %get-tuple-element.354, f32[1,8]{0,1:T(8,128)S(1)} %get-tuple-element.355, f32[1,8]{0,1:T(8,128)S(1)} %get-tuple-element.356, f32[]{:T(128)} %bitcast.67, f32[]{:T(128)S(6)} %mul.2504, f32[]{:T(128)} %bitcast.81, ...), kind=kLoop, calls=%fused_computation.361 | loop fusion | flops 960 | bytes 432 | tf_op jit(solution)/shard_map/div | solution.py:152
  590.5 12.6 %subtract_divide_fusion.7 = f32[1,8]{0,1:T(8,128)S(1)} fusion(f32[1,8]{0,1:T(8,128)S(1)} %get-tuple-element.353, f32[1,8]{0,1:T(8,128)S(1)} %get-tuple-element.354, f32[1,8]{0,1:T(8,128)S(1)} %get-tuple-element.355, f32[1,8]{0,1:T(8,128)S(1)} %get-tuple-element.356, f32[8,8]{0,1:T(8,128)S(1)} %fusion.251, f32[]{:T(128)} %bitcast.51, f32[]{:T(128)} %bitcast.31, ...), kind=kLoop, calls=%fused_computation.368 | loop fusion | flops 320 | bytes 288 | tf_op jit(solution)/shard_map/div | solution.py:151
  603.0 19.2 %subtract_divide_fusion.5 = f32[1,8]{0,1:T(8,128)S(1)} fusion(f32[1,8]{0,1:T(8,128)S(1)} %get-tuple-element.354, f32[1,8]{0,1:T(8,128)S(1)} %get-tuple-element.355, f32[1,8]{0,1:T(8,128)S(1)} %get-tuple-element.356, f32[1,8]{0,1:T(8,128)S(1)} %get-tuple-element.353, f32[8,8]{0,1:T(8,128)S(1)} %fusion.251, f32[]{:T(128)} %bitcast.65, f32[]{:T(128)} %bitcast.41, ...), kind=kLoop, calls=%fused_computation.365 | loop fusion | flops 608 | bytes 372 | tf_op jit(solution)/shard_map/div | solution.py:151
  622.3 27.2 %subtract_divide_fusion.3 = f32[1,8]{0,1:T(8,128)S(1)} fusion(f32[]{:T(128)} %bitcast.81, f32[1,8]{0,1:T(8,128)S(1)} %get-tuple-element.353, f32[1,8]{0,1:T(8,128)S(1)} %get-tuple-element.354, f32[1,8]{0,1:T(8,128)S(1)} %get-tuple-element.355, f32[1,8]{0,1:T(8,128)S(1)} %get-tuple-element.356, f32[]{:T(128)} %bitcast.53, f32[8,8]{0,1:T(8,128)S(1)} %fusion.251, ...), kind=kLoop, calls=%fused_computation.362 | loop fusion | flops 960 | bytes 464 | tf_op jit(solution)/shard_map/div | solution.py:151
  649.5 36.8 %subtract_divide_fusion = f32[1,8]{0,1:T(8,128)S(1)} fusion(f32[1,8]{0,1:T(8,128)S(1)} %get-tuple-element.353, f32[1,8]{0,1:T(8,128)S(1)} %get-tuple-element.354, f32[1,8]{0,1:T(8,128)S(1)} %get-tuple-element.355, f32[1,8]{0,1:T(8,128)S(1)} %get-tuple-element.356, f32[]{:T(128)} %bitcast.83, f32[]{:T(128)S(6)} %mul.2550, f32[]{:T(128)} %bitcast.99, ...), kind=kLoop, calls=%fused_computation.359 | loop fusion | flops 1376 | bytes 532 | tf_op jit(solution)/shard_map/div | solution.py:152
  (318 shorter events, 200.0 us)
Async XLA Ops:
  7.2 372.1 %all-gather.2.cloned.1.call-start = ((), (), s32[]{:S(2)}) async-start(), calls=%async_computation | async-start | bytes 17825792 | tf_op jit(solution)/shard_map/all_gather | solution.py:229
  8.5 16.8 %collective-permute-start.1 = (f32[4,2,64,256]{3,2,1,0:T(8,128)S(1)}, f32[4,2,64,256]{3,2,1,0:T(8,128)S(1)}, u32[]{:S(2)}, u32[]{:S(2)}) collective-permute-start(f32[4,2,64,256]{3,2,1,0:T(8,128)S(1)} %get-tuple-element.393), channel_id=1, source_target_pairs={{2,0},{4,2},{6,4},{8,6},{10,8},{12,10},{14,12},{3,1},{5,3},{7,5},{... | collective-permute-start | bytes 1572872 | tf_op jit(solution)/shard_map/ppermute | solution.py:24
  9.8 26.8 %collective-permute-start = (f32[4,2,64,256]{3,2,1,0:T(8,128)S(1)}, f32[4,2,64,256]{3,2,1,0:T(8,128)}, u32[]{:S(2)}, u32[]{:S(2)}) collective-permute-start(f32[4,2,64,256]{3,2,1,0:T(8,128)S(1)} %get-tuple-element.392), channel_id=1, source_target_pairs={{0,2},{2,4},{4,6},{6,8},{8,10},{10,12},{12,14},{1,3},{3,5},{5,7},{... | collective-permute-start | bytes 1572872 | tf_op jit(solution)/shard_map/ppermute | solution.py:23
  25.6 19.8 %copy-start.18 = (s32[2,2]{1,0:T(2,128)S(1)}, s32[2,2]{1,0:T(2,128)}, u32[]{:S(2)}) copy-start(s32[2,2]{1,0:T(2,128)} %param.11) | copy-start | bytes 52
  38.0 7.4 %copy-start.9 = (f32[4,2,64,256]{2,3,1,0:T(8,128)}, f32[4,2,64,256]{2,3,1,0:T(8,128)S(1)}, u32[]{:S(2)}) copy-start(f32[4,2,64,256]{2,3,1,0:T(8,128)S(1)} %copy.329) | copy-start | bytes 1572868
  38.1 8.9 %copy-start.19 = (f32[2,63]{1,0:T(2,128)S(1)}, f32[2,63]{1,0:T(2,128)}, u32[]{:S(2)}) copy-start(f32[2,63]{1,0:T(2,128)} %param.9) | copy-start | bytes 1516
  39.5 14.0 %collective-permute-start.3 = (f32[4,2,256,64]{2,3,1,0:T(8,128)}, f32[4,2,256,64]{2,3,1,0:T(8,128)}, u32[]{:S(2)}, u32[]{:S(2)}) collective-permute-start(f32[4,2,256,64]{2,3,1,0:T(8,128)} %get-tuple-element.389), channel_id=1, source_target_pairs={{1,0},{3,2},{5,4},{7,6},{9,8},{11,10},{13,12},{15,14},{17,16},{19,... | collective-permute-start | bytes 1572872 | tf_op jit(solution)/shard_map/ppermute | solution.py:24
  40.8 12.7 %collective-permute-start.2 = (f32[4,2,256,64]{2,3,1,0:T(8,128)}, f32[4,2,256,64]{2,3,1,0:T(8,128)}, u32[]{:S(2)}, u32[]{:S(2)}) collective-permute-start(f32[4,2,256,64]{2,3,1,0:T(8,128)} %get-tuple-element.388), channel_id=1, source_target_pairs={{0,1},{2,3},{4,5},{6,7},{8,9},{10,11},{12,13},{14,15},{16,17},{18,... | collective-permute-start | bytes 1572872 | tf_op jit(solution)/shard_map/ppermute | solution.py:23
  47.0 6.6 copy-start.10
  59.7 9.6 %copy-start = (f32[8,2,128,128]{2,3,0,1:T(8,128)}, f32[8,2,128,128]{2,3,0,1:T(8,128)S(1)}, u32[]{:S(2)}) copy-start(f32[8,2,128,128]{2,3,0,1:T(8,128)S(1)} %get-tuple-element.634) | copy-start | bytes 3145732 | tf_op jit(solution)/shard_map/while
  66.5 3.4 copy-start.4
  66.5 3.4 copy-start.6
  92.8 5.5 copy-start.2
  92.8 5.5 copy-start.3
  99.5 4.6 copy-start.17
  124.5 3.2 copy-start.1
  124.5 3.2 copy-start.5
  139.9 9.6 %copy-start = (f32[8,2,128,128]{2,3,0,1:T(8,128)}, f32[8,2,128,128]{2,3,0,1:T(8,128)S(1)}, u32[]{:S(2)}) copy-start(f32[8,2,128,128]{2,3,0,1:T(8,128)S(1)} %get-tuple-element.634) | copy-start | bytes 3145732 | tf_op jit(solution)/shard_map/while
  146.8 3.4 copy-start.4
  146.8 3.4 copy-start.6
  173.2 5.5 copy-start.2
  173.2 5.5 copy-start.3
  179.9 4.6 copy-start.17
  205.0 3.2 copy-start.1
  205.0 3.2 copy-start.5
  205.0 3.2 copy-start.7
  229.0 5.1 copy-start.8
  234.3 31.6 %collective-permute-start.5 = (f32[4,2,64,384]{3,2,1,0:T(8,128)S(1)}, f32[4,2,64,384]{3,2,1,0:T(8,128)S(1)}, u32[]{:S(2)}, u32[]{:S(2)}) collective-permute-start(f32[4,2,64,384]{3,2,1,0:T(8,128)S(1)} %get-tuple-element.387), channel_id=1, source_target_pairs={{2,0},{4,2},{6,4},{8,6},{10,8},{12,10},{14,12},{3,1},{5,3},{7,5},{... | collective-permute-start | bytes 2359304 | tf_op jit(solution)/shard_map/ppermute | solution.py:13
  235.6 52.9 %copy-start.16 = (f32[8,2,128,128]{3,2,1,0:T(8,128)S(1)}, f32[8,2,128,128]{3,2,1,0:T(8,128)}, u32[]{:S(2)}) copy-start(f32[8,2,128,128]{3,2,1,0:T(8,128)} %param.8) | copy-start | bytes 3145732
  235.6 48.1 %collective-permute-start.4 = (f32[4,2,64,384]{3,2,1,0:T(8,128)S(1)}, f32[4,2,64,384]{3,2,1,0:T(8,128)S(1)}, u32[]{:S(2)}, u32[]{:S(2)}) collective-permute-start(f32[4,2,64,384]{3,2,1,0:T(8,128)S(1)} %get-tuple-element.386), channel_id=1, source_target_pairs={{0,2},{2,4},{4,6},{6,8},{8,10},{10,12},{12,14},{1,3},{3,5},{5,7},{... | collective-permute-start | bytes 2359304 | tf_op jit(solution)/shard_map/ppermute | solution.py:13
  284.1 5.1 collective-permute-start.7
  285.4 4.6 collective-permute-start.6
  (10 other events, 25.9 us)
Sparse Core Ops, SparseCore 0:
  234.3 144.9 all-gather.1
